TPU v7x, 32 devices: a whole 2x2x4 slice. The times are simulated.
32 devices in a mesh: gx: 4 (over y, x), gy: 2 (over core), gz: 4 (over z).
Axes of the slice: x: 2, y: 2, z: 4, core: 2. Of those that a mesh axis runs over, the one named last changes fastest.
Arguments:
- fields: float32 [64, 8, 16, 256], P(('gx', 'gy', 'gz')), may hold values from 0 to 1
- seed_labels: int32 [64, 256], P(('gx', 'gy', 'gz')), may hold values from 0 to 3
- coords: int32 [48, 3], replicated, may hold values from 0 to 5, as said below
- neighbours: int32 [48, 6], replicated, may hold values from -1 to 47, as said below
- owner_before: int32 [48], replicated, may hold values from 0 to 63, as said below
- owner_after: int32 [48], replicated, may hold values from 0 to 63, as said below
- couple: float32 [4, 4], replicated, may hold values from -3 to 3
- latent: float32 [4, 4], replicated, may hold values from -3 to 3
- diffuse: float32 [4], replicated, may hold values from 0.3 to 1.5
- thermal_gain: float32 [4], replicated, may hold values from -4 to 4
Outputs:
- fields_out: float32 [64, 8, 16, 256], P(('gx', 'gy', 'gz'))
Inputs may be any that keep to these rules, and one draw needn't show every extreme that they name: `coords`: a permutation of the positions of a 4 x 2 x 6 grid of blocks. `neighbours`: the block beside b across each side by coords; -1 beyond the ends along x and y; along z the blocks close into a loop. `owner_before`: distinct for distinct blocks; a place p is slot p % 2 of device p // 2, devices counted over gx, gy, gz in order; block b's device has index coords[b, 0] along gx and coords[b, 1] along gy. `owner_after`: distinct for distinct blocks; a block's device after migration is its device before or the next one along gz, cyclic, with the same gx and gy indices; at most one block of a device moves; in every group of devices along gz at least one block moves.
All inputs are finite; a program needn't handle non-finite values.
Results may differ from a plain program's by a relative error of at most 0.0003.
Values sent between devices are 32-bit elements; how exact they have to be, the bound alone decides.
A program may use at most 64 MiB of HBM per device.

v0:
```python
import jax
import jax.numpy as jnp
from jax import lax
from jax.sharding import PartitionSpec as P

CB = 16
NPHASE = 4
SLOTS = 2
STEPS = 2


seed_gain = 2.0


def passed_along(block, axis, distance):
    devices = range(lax.axis_size(axis))
    route = [(i - distance, i) for i in devices if i - distance in devices]
    return lax.ppermute(block, axis, route)


def from_behind(value, axis, steps):
    count = lax.axis_size(axis)
    pairs = [(source, (source + steps) % count) for source in range(count)]
    return lax.ppermute(value, axis, pairs)


def faces_of(volume):
    components, extent, surface = volume.shape
    low_x = volume[:, 0, :]
    high_x = volume[:, extent - 1, :]
    low_y = volume[:, :, :extent].reshape(components, extent * extent)
    high_y = volume[:, :, surface - extent :].reshape(components, extent * extent)
    low_z = volume[:, :, 0::extent].reshape(components, extent * extent)
    high_z = volume[:, :, extent - 1 :: extent].reshape(components, extent * extent)
    return jnp.stack([low_x, high_x, low_y, high_y, low_z, high_z], 0)


def laplace(volume, ghosts):
    components, extent, surface = volume.shape
    below_x = jnp.concatenate([ghosts[0][:, None, :], volume[:, :-1, :]], 1)
    above_x = jnp.concatenate([volume[:, 1:, :], ghosts[1][:, None, :]], 1)
    below_y = jnp.concatenate(
        [ghosts[2].reshape(components, extent, extent), volume[:, :, :-extent]], 2
    )
    above_y = jnp.concatenate(
        [volume[:, :, extent:], ghosts[3].reshape(components, extent, extent)], 2
    )
    offset_z = jnp.arange(surface) % extent
    zeros_col = jnp.zeros((components, extent, 1), volume.dtype)
    below_z = jnp.where(
        offset_z == 0,
        jnp.repeat(ghosts[4].reshape(components, extent, extent), extent, axis=2),
        jnp.concatenate([zeros_col, volume[:, :, :-1]], 2),
    )
    above_z = jnp.where(
        offset_z == extent - 1,
        jnp.repeat(ghosts[5].reshape(components, extent, extent), extent, axis=2),
        jnp.concatenate([volume[:, :, 1:], zeros_col], 2),
    )
    return below_x + above_x + below_y + above_y + below_z + above_z - 6.0 * volume


def phase_step(
    phases, potential, ghosts, x_global, seed_row, iteration, couple, thermal_gain, seeded
):
    extent = phases.shape[1]
    thermal = x_global / (2.0 * extent) - 1.0 - 0.25 * iteration
    driving = jnp.einsum("kj,jxc->kxc", couple, potential, precision=lax.Precision.HIGHEST)
    driving = driving + thermal_gain[:, None, None] * thermal[None, :, None]
    if seeded:
        marks = (
            seed_row[None, None, :] == jnp.arange(phases.shape[0], dtype=jnp.int32)[:, None, None]
        )
        driving = driving + seed_gain * marks.astype(jnp.float32)
    return (
        phases + 0.12 * laplace(phases, ghosts) + phases * (1.0 - phases) * (phases - 0.5 + driving)
    )


def potential_step(potential, ghosts, old_phases, new_phases, diffuse, latent):
    release = jnp.einsum(
        "jk,kxc->jxc", latent, new_phases - old_phases, precision=lax.Precision.HIGHEST
    )
    return potential + 0.1 * diffuse[:, None, None] * laplace(potential, ghosts) - release


def holdings(owners, slot_ids):
    matches = owners[None, :] == slot_ids[:, None]
    filled = jnp.any(matches, 1)
    holder = jnp.sum(
        jnp.where(matches, jnp.arange(owners.shape[0], dtype=jnp.int32)[None, :], 0), 1
    )
    return (holder, filled)


def route(values, owners, holder, filled, neighbours, linear, cycle_pos, cycle_len):
    outgoing = jax.vmap(faces_of)(values)
    targets = neighbours[holder]
    slot_range = jnp.arange(SLOTS, dtype=jnp.int32)
    valid = jnp.logical_and(filled[:, None], targets >= 0)
    dest_place = owners[jnp.maximum(targets, 0)]
    cycle_dest = dest_place // SLOTS % cycle_len
    cycle_range = jnp.arange(cycle_len, dtype=jnp.int32)
    chosen = jnp.logical_and(
        jnp.logical_and(
            valid[None, None], cycle_dest[None, None] == cycle_range[:, None, None, None]
        ),
        (dest_place % SLOTS)[None, None] == slot_range[None, :, None, None],
    ).astype(jnp.float32)
    outbound = jnp.einsum("gtse,sefc->gtefc", chosen, outgoing, precision=lax.Precision.HIGHEST)
    inbound = lax.all_to_all(outbound, "gz", split_axis=0, concat_axis=0, tiled=True)
    routed = jnp.sum(inbound, 0)
    lower_x = passed_along(routed[:, 1], "gx", 1)
    upper_x = passed_along(routed[:, 0], "gx", -1)
    lower_y = passed_along(routed[:, 3], "gy", 1)
    upper_y = passed_along(routed[:, 2], "gy", -1)
    incoming = jnp.stack([lower_x, upper_x, lower_y, upper_y, routed[:, 5], routed[:, 4]], 1)
    return jnp.where((targets >= 0)[:, :, None, None], incoming, outgoing)


def migrate(
    phases,
    potential,
    holder,
    filled,
    owner_before,
    owner_after,
    linear,
    cycle_pos,
    cycle_len,
    my_slots,
):
    stacked = jnp.concatenate([phases, potential], 1)
    prior = linear - cycle_pos + (cycle_pos + cycle_len - 1) % cycle_len
    prior_slots = prior * SLOTS + jnp.arange(SLOTS, dtype=jnp.int32)
    prior_ids, prior_full = holdings(owner_before, prior_slots)
    arrived = from_behind(stacked, "gz", 1)
    candidates = jnp.concatenate([stacked, arrived], 0)
    cand_ids = jnp.concatenate([holder, prior_ids], 0)
    cand_full = jnp.concatenate([filled, prior_full], 0)
    weights = jnp.logical_and(
        cand_full[None, :], owner_after[cand_ids][None, :] == my_slots[:, None]
    ).astype(jnp.float32)
    placed = jnp.einsum("tc,cfxp->tfxp", weights, candidates, precision=lax.Precision.HIGHEST)
    new_holder, new_filled = holdings(owner_after, my_slots)
    return (placed[:, :NPHASE], placed[:, NPHASE:], new_holder, new_filled)


def per_device(
    fields,
    seed_labels,
    coords,
    neighbours,
    owner_before,
    owner_after,
    couple,
    latent,
    diffuse,
    thermal_gain,
):
    cycle_len = lax.axis_size("gz")
    cycle_pos = lax.axis_index("gz")
    linear = (
        lax.axis_index("gx") * lax.axis_size("gy") + lax.axis_index("gy")
    ) * cycle_len + cycle_pos
    my_slots = linear * SLOTS + jnp.arange(SLOTS, dtype=jnp.int32)
    owners = owner_before
    holder, filled = holdings(owners, my_slots)
    phases = fields[:, :NPHASE]
    potential = fields[:, NPHASE:]
    for iteration in range(STEPS):
        if iteration == STEPS // 2:
            phases, potential, holder, filled = migrate(
                phases,
                potential,
                holder,
                filled,
                owner_before,
                owner_after,
                linear,
                cycle_pos,
                cycle_len,
                my_slots,
            )
            owners = owner_after
        x_global = (coords[holder][:, 0:1] * CB + jnp.arange(CB, dtype=jnp.int32)[None, :]).astype(
            jnp.float32
        )
        ghosts = route(
            jnp.concatenate([phases, potential], 1),
            owners,
            holder,
            filled,
            neighbours,
            linear,
            cycle_pos,
            cycle_len,
        )
        phase_ghost = ghosts[:, :, :NPHASE]
        pot_ghost = ghosts[:, :, NPHASE:]
        new_phases = jax.vmap(
            lambda phase_one, pot_one, ghost_one, xpos_one, seed_one: phase_step(
                phase_one,
                pot_one,
                ghost_one,
                xpos_one,
                seed_one,
                iteration,
                couple,
                thermal_gain,
                iteration == 0,
            )
        )(phases, potential, phase_ghost, x_global, seed_labels)
        potential = jax.vmap(
            lambda pot_one, ghost_one, old_one, new_one: potential_step(
                pot_one, ghost_one, old_one, new_one, diffuse, latent
            )
        )(potential, pot_ghost, phases, new_phases)
        phases = new_phases
    result = jnp.concatenate([phases, potential], 1)
    return result * filled.astype(jnp.float32)[:, None, None, None]


def solution(mesh):
    placed = (
        P(("gx", "gy", "gz"), None, None, None),
        P(("gx", "gy", "gz"), None),
        P(),
        P(),
        P(),
        P(),
        P(),
        P(),
        P(),
        P(),
    )
    return jax.shard_map(
        per_device,
        mesh=mesh,
        in_specs=placed,
        out_specs=P(("gx", "gy", "gz"), None, None, None),
        check_vma=False,
    )
```

profile of v0, /device:TPU:5, one launch (start us, length us, event | category | flops | bytes accessed | tf_op | source)
XLA Modules:
  0.0 102.7 jit_solution(3022237333636106049)
XLA Ops:
  1.6 1.0 fusion.87
  2.6 1.1 %fusion.86 = (f32[2,8,16,16]{3,2,1,0:T(8,128)S(1)}, f32[2,8,16,16]{3,2,1,0:T(8,128)S(1)}) fusion(f32[2,8,16,256]{3,2,1,0:T(8,128)} %param.10), kind=kLoop, calls=%fused_computation.212 | loop fusion | bytes 65536 | tf_op jit(solution)/shard_map/vmap()/slice | solution.py:32
  4.5 0.8 slice.296
  9.2 0.9 copy.264
  10.1 4.6 %all-to-all-start = ((f32[4,2,6,8,256]{4,1,3,2,0:T(2,128)}), f32[4,2,6,8,256]{4,1,3,2,0:T(2,128)S(1)}, u32[]{:S(2)}, u32[]{:S(2)}) async-start(f32[4,2,6,8,256]{4,1,3,2,0:T(2,128)} %copy.264), calls=%async_computation | async-start | bytes 786432 | tf_op jit(solution)/shard_map/all_to_all | solution.py:111
  22.5 3.5 %all-to-all-done = f32[4,2,6,8,256]{4,1,3,2,0:T(2,128)S(1)} async-done(((f32[4,2,6,8,256]{4,1,3,2,0:T(2,128)}), f32[4,2,6,8,256]{4,1,3,2,0:T(2,128)S(1)}, u32[]{:S(2)}, u32[]{:S(2)}) %all-to-all-start) | async-done | bytes 393248 | tf_op jit(solution)/shard_map/all_to_all | solution.py:111
  26.2 3.1 %collective-permute-start = (f32[2,8,256]{2,0,1:T(2,128)S(1)}, f32[2,8,256]{2,0,1:T(2,128)S(1)}, u32[]{:S(2)}, u32[]{:S(2)}) collective-permute-start(f32[2,8,256]{2,0,1:T(2,128)S(1)} %get-tuple-element.84), channel_id=1, source_target_pairs={{0,8},{8,16},{16,24},{1,9},{9,17},{17,25},{2,10},{10,18},{18,26},{... | collective-permute-start | bytes 49160 | tf_op jit(solution)/shard_map/ppermute | solution.py:18
  31.1 3.1 %collective-permute-start.1 = (f32[2,8,256]{2,0,1:T(2,128)S(1)}, f32[2,8,256]{2,0,1:T(2,128)S(1)}, u32[]{:S(2)}, u32[]{:S(2)}) collective-permute-start(f32[2,8,256]{2,0,1:T(2,128)S(1)} %get-tuple-element.83), channel_id=1, source_target_pairs={{8,0},{16,8},{24,16},{9,1},{17,9},{25,17},{10,2},{18,10},{26,18},{... | collective-permute-start | bytes 49160 | tf_op jit(solution)/shard_map/ppermute | solution.py:18
  34.2 1.3 %collective-permute-start.2 = (f32[2,8,256]{2,0,1:T(2,128)S(1)}, f32[2,8,256]{2,0,1:T(2,128)S(1)}, u32[]{:S(2)}, u32[]{:S(2)}) collective-permute-start(f32[2,8,256]{2,0,1:T(2,128)S(1)} %get-tuple-element.82), channel_id=1, source_target_pairs={{0,4},{1,5},{2,6},{3,7},{8,12},{9,13},{10,14},{11,15},{16,20},{17,... | collective-permute-start | bytes 49160 | tf_op jit(solution)/shard_map/ppermute | solution.py:18
  35.5 3.9 %collective-permute-start.3 = (f32[2,8,256]{2,0,1:T(2,128)S(1)}, f32[2,8,256]{2,0,1:T(2,128)S(1)}, u32[]{:S(2)}, u32[]{:S(2)}) collective-permute-start(f32[2,8,256]{2,0,1:T(2,128)S(1)} %get-tuple-element.81), channel_id=1, source_target_pairs={{4,0},{5,1},{6,2},{7,3},{12,8},{13,9},{14,10},{15,11},{20,16},{21,... | collective-permute-start | bytes 49160 | tf_op jit(solution)/shard_map/ppermute | solution.py:18
  39.4 0.8 collective-permute-done.3
  53.5 4.2 %collective-permute-done.4 = f32[2,8,16,256]{3,1,2,0:T(8,128)S(1)} collective-permute-done((f32[2,8,16,256]{3,1,2,0:T(8,128)S(1)}, f32[2,8,16,256]{3,1,2,0:T(8,128)S(1)}, u32[]{:S(2)}, u32[]{:S(2)}) %collective-permute-start.4) | collective-permute-done | bytes 262176 | tf_op jit(solution)/shard_map/ppermute | solution.py:24
  57.8 0.9 fusion.11
  58.9 1.4 %slice.334 = f32[2,8,16,16]{3,0,2,1:T(2,128)S(1)} slice(f32[2,8,16,256]{3,0,2,1:T(2,128)S(1)} %fusion.11), slice={[0:2:1], [0:8:1], [0:16:1], [0:256:16]} | slice | bytes 32768 | tf_op jit(solution)/shard_map/vmap()/slice | solution.py:33
  60.4 1.5 %slice.335 = f32[2,8,16,16]{3,0,2,1:T(2,128)S(1)} slice(f32[2,8,16,256]{3,0,2,1:T(2,128)S(1)} %fusion.11), slice={[0:2:1], [0:8:1], [0:16:1], [15:256:16]} | slice | bytes 32768 | tf_op jit(solution)/shard_map/vmap()/slice | solution.py:34
  63.1 0.9 copy.305
  64.0 3.5 %all-to-all-start.1 = ((f32[4,2,6,8,256]{4,1,3,2,0:T(2,128)}), f32[4,2,6,8,256]{4,1,3,2,0:T(2,128)S(1)}, u32[]{:S(2)}, u32[]{:S(2)}) async-start(f32[4,2,6,8,256]{4,1,3,2,0:T(2,128)} %copy.305), calls=%async_computation.1 | async-start | bytes 786432 | tf_op jit(solution)/shard_map/all_to_all | solution.py:111
  68.3 10.4 %all-to-all-done.1 = f32[4,2,6,8,256]{4,1,3,2,0:T(2,128)S(1)} async-done(((f32[4,2,6,8,256]{4,1,3,2,0:T(2,128)}), f32[4,2,6,8,256]{4,1,3,2,0:T(2,128)S(1)}, u32[]{:S(2)}, u32[]{:S(2)}) %all-to-all-start.1) | async-done | bytes 393248 | tf_op jit(solution)/shard_map/all_to_all | solution.py:111
  78.9 2.2 %collective-permute-start.5 = (f32[2,8,256]{2,1,0:T(8,128)S(1)}, f32[2,8,256]{2,1,0:T(8,128)S(1)}, u32[]{:S(2)}, u32[]{:S(2)}) collective-permute-start(f32[2,8,256]{2,1,0:T(8,128)S(1)} %bitcast.241), channel_id=1, source_target_pairs={{0,8},{8,16},{16,24},{1,9},{9,17},{17,25},{2,10},{10,18},{18,26},{... | collective-permute-start | bytes 49160 | tf_op jit(solution)/shard_map/ppermute | solution.py:18
  83.4 4.0 %collective-permute-start.6 = (f32[2,8,256]{2,1,0:T(8,128)S(1)}, f32[2,8,256]{2,1,0:T(8,128)S(1)}, u32[]{:S(2)}, u32[]{:S(2)}) collective-permute-start(f32[2,8,256]{2,1,0:T(8,128)S(1)} %bitcast.244), channel_id=1, source_target_pairs={{8,0},{16,8},{24,16},{9,1},{17,9},{25,17},{10,2},{18,10},{26,18},{... | collective-permute-start | bytes 49160 | tf_op jit(solution)/shard_map/ppermute | solution.py:18
  87.4 1.3 %collective-permute-start.7 = (f32[2,8,256]{2,1,0:T(8,128)S(1)}, f32[2,8,256]{2,1,0:T(8,128)S(1)}, u32[]{:S(2)}, u32[]{:S(2)}) collective-permute-start(f32[2,8,256]{2,1,0:T(8,128)S(1)} %bitcast.243), channel_id=1, source_target_pairs={{0,4},{1,5},{2,6},{3,7},{8,12},{9,13},{10,14},{11,15},{16,20},{17,... | collective-permute-start | bytes 49160 | tf_op jit(solution)/shard_map/ppermute | solution.py:18
  88.7 3.9 %collective-permute-start.8 = (f32[2,8,256]{2,1,0:T(8,128)S(1)}, f32[2,8,256]{2,1,0:T(8,128)S(1)}, u32[]{:S(2)}, u32[]{:S(2)}) collective-permute-start(f32[2,8,256]{2,1,0:T(8,128)S(1)} %bitcast.242), channel_id=1, source_target_pairs={{4,0},{5,1},{6,2},{7,3},{12,8},{13,9},{14,10},{15,11},{20,16},{21,... | collective-permute-start | bytes 49160 | tf_op jit(solution)/shard_map/ppermute | solution.py:18
  92.6 0.8 collective-permute-done.8
  101.9 0.8 copy.338
  (275 shorter events, 41.7 us)
Async XLA Ops:
  0.0 46.0 %copy-start = (f32[4,4]{1,0:T(4,128)S(1)}, f32[4,4]{1,0:T(4,128)}, u32[]{:S(2)}) copy-start(f32[4,4]{1,0:T(4,128)} %param.16) | copy-start | bytes 196
  1.6 5.0 %copy-start.18 = (pred[2]{0:T(512)(128)(4,1)}, pred[2]{0:T(512)(128)(4,1)S(1)}, u32[]{:S(2)}) copy-start(pred[2]{0:T(512)(128)(4,1)S(1)} %get-tuple-element.6) | copy-start | bytes 10
  1.6 17.8 %copy-start.16 = (pred[2]{0:T(512)(128)(4,1)}, pred[2]{0:T(512)(128)(4,1)S(1)}, u32[]{:S(2)}) copy-start(pred[2]{0:T(512)(128)(4,1)S(1)} %get-tuple-element.5) | copy-start | bytes 10
  2.6 1.1 %copy-start.3 = (f32[2,8,16,256]{3,2,1,0:T(8,128)S(1)}, f32[2,8,16,256]{3,2,1,0:T(8,128)}, u32[]{:S(2)}) copy-start(f32[2,8,16,256]{3,2,1,0:T(8,128)} %param.10) | copy-start | bytes 786436
  10.1 15.8 %all-to-all-start = ((f32[4,2,6,8,256]{4,1,3,2,0:T(2,128)}), f32[4,2,6,8,256]{4,1,3,2,0:T(2,128)S(1)}, u32[]{:S(2)}, u32[]{:S(2)}) async-start(f32[4,2,6,8,256]{4,1,3,2,0:T(2,128)} %copy.264), calls=%async_computation | async-start | bytes 786432 | tf_op jit(solution)/shard_map/all_to_all | solution.py:111
  26.2 13.2 %collective-permute-start = (f32[2,8,256]{2,0,1:T(2,128)S(1)}, f32[2,8,256]{2,0,1:T(2,128)S(1)}, u32[]{:S(2)}, u32[]{:S(2)}) collective-permute-start(f32[2,8,256]{2,0,1:T(2,128)S(1)} %get-tuple-element.84), channel_id=1, source_target_pairs={{0,8},{8,16},{16,24},{1,9},{9,17},{17,25},{2,10},{10,18},{18,26},{... | collective-permute-start | bytes 49160 | tf_op jit(solution)/shard_map/ppermute | solution.py:18
  31.1 8.3 %collective-permute-start.1 = (f32[2,8,256]{2,0,1:T(2,128)S(1)}, f32[2,8,256]{2,0,1:T(2,128)S(1)}, u32[]{:S(2)}, u32[]{:S(2)}) collective-permute-start(f32[2,8,256]{2,0,1:T(2,128)S(1)} %get-tuple-element.83), channel_id=1, source_target_pairs={{8,0},{16,8},{24,16},{9,1},{17,9},{25,17},{10,2},{18,10},{26,18},{... | collective-permute-start | bytes 49160 | tf_op jit(solution)/shard_map/ppermute | solution.py:18
  34.2 5.2 %collective-permute-start.2 = (f32[2,8,256]{2,0,1:T(2,128)S(1)}, f32[2,8,256]{2,0,1:T(2,128)S(1)}, u32[]{:S(2)}, u32[]{:S(2)}) collective-permute-start(f32[2,8,256]{2,0,1:T(2,128)S(1)} %get-tuple-element.82), channel_id=1, source_target_pairs={{0,4},{1,5},{2,6},{3,7},{8,12},{9,13},{10,14},{11,15},{16,20},{17,... | collective-permute-start | bytes 49160 | tf_op jit(solution)/shard_map/ppermute | solution.py:18
  35.5 4.7 %collective-permute-start.3 = (f32[2,8,256]{2,0,1:T(2,128)S(1)}, f32[2,8,256]{2,0,1:T(2,128)S(1)}, u32[]{:S(2)}, u32[]{:S(2)}) collective-permute-start(f32[2,8,256]{2,0,1:T(2,128)S(1)} %get-tuple-element.81), channel_id=1, source_target_pairs={{4,0},{5,1},{6,2},{7,3},{12,8},{13,9},{14,10},{15,11},{20,16},{21,... | collective-permute-start | bytes 49160 | tf_op jit(solution)/shard_map/ppermute | solution.py:18
  45.8 0.8 copy-start.6
  45.9 0.8 copy-start.12
  46.7 0.8 copy-start.27
  48.2 9.6 %collective-permute-start.4 = (f32[2,8,16,256]{3,1,2,0:T(8,128)S(1)}, f32[2,8,16,256]{3,1,2,0:T(8,128)S(1)}, u32[]{:S(2)}, u32[]{:S(2)}) collective-permute-start(f32[2,8,16,256]{3,1,2,0:T(8,128)S(1)} %pad_maximum_fusion.1), channel_id=1, source_target_pairs={{0,1},{1,2},{2,3},{3,0},{4,5},{5,6},{6,7},{7,4},{8,9},{9,10},{10,1... | collective-permute-start | bytes 786440 | tf_op jit(solution)/shard_map/ppermute | solution.py:24
  64.0 14.7 %all-to-all-start.1 = ((f32[4,2,6,8,256]{4,1,3,2,0:T(2,128)}), f32[4,2,6,8,256]{4,1,3,2,0:T(2,128)S(1)}, u32[]{:S(2)}, u32[]{:S(2)}) async-start(f32[4,2,6,8,256]{4,1,3,2,0:T(2,128)} %copy.305), calls=%async_computation.1 | async-start | bytes 786432 | tf_op jit(solution)/shard_map/all_to_all | solution.py:111
  78.9 13.6 %collective-permute-start.5 = (f32[2,8,256]{2,1,0:T(8,128)S(1)}, f32[2,8,256]{2,1,0:T(8,128)S(1)}, u32[]{:S(2)}, u32[]{:S(2)}) collective-permute-start(f32[2,8,256]{2,1,0:T(8,128)S(1)} %bitcast.241), channel_id=1, source_target_pairs={{0,8},{8,16},{16,24},{1,9},{9,17},{17,25},{2,10},{10,18},{18,26},{... | collective-permute-start | bytes 49160 | tf_op jit(solution)/shard_map/ppermute | solution.py:18
  83.4 9.2 %collective-permute-start.6 = (f32[2,8,256]{2,1,0:T(8,128)S(1)}, f32[2,8,256]{2,1,0:T(8,128)S(1)}, u32[]{:S(2)}, u32[]{:S(2)}) collective-permute-start(f32[2,8,256]{2,1,0:T(8,128)S(1)} %bitcast.244), channel_id=1, source_target_pairs={{8,0},{16,8},{24,16},{9,1},{17,9},{25,17},{10,2},{18,10},{26,18},{... | collective-permute-start | bytes 49160 | tf_op jit(solution)/shard_map/ppermute | solution.py:18
  87.4 5.2 %collective-permute-start.7 = (f32[2,8,256]{2,1,0:T(8,128)S(1)}, f32[2,8,256]{2,1,0:T(8,128)S(1)}, u32[]{:S(2)}, u32[]{:S(2)}) collective-permute-start(f32[2,8,256]{2,1,0:T(8,128)S(1)} %bitcast.243), channel_id=1, source_target_pairs={{0,4},{1,5},{2,6},{3,7},{8,12},{9,13},{10,14},{11,15},{16,20},{17,... | collective-permute-start | bytes 49160 | tf_op jit(solution)/shard_map/ppermute | solution.py:18
  88.7 4.7 %collective-permute-start.8 = (f32[2,8,256]{2,1,0:T(8,128)S(1)}, f32[2,8,256]{2,1,0:T(8,128)S(1)}, u32[]{:S(2)}, u32[]{:S(2)}) collective-permute-start(f32[2,8,256]{2,1,0:T(8,128)S(1)} %bitcast.242), channel_id=1, source_target_pairs={{4,0},{5,1},{6,2},{7,3},{12,8},{13,9},{14,10},{15,11},{20,16},{21,... | collective-permute-start | bytes 49160 | tf_op jit(solution)/shard_map/ppermute | solution.py:18
  98.8 0.9 copy-start.5
  98.8 0.9 copy-start.4
  98.9 0.8 copy-start.10
  99.0 0.8 copy-start.9
  99.0 0.8 copy-start.33
  99.0 0.8 copy-start.35
  (23 other events, 15.6 us)
where the time goes:
time: 103 us
  local copies, waits for them, and re-layouts  39.8 us (39%)
  starting transfers between devices  31 us (30%)
  waiting for transfers between devices  19.6 us (19%)
  other arithmetic  6.16 us (6%)
  matrix products  4.83 us (5%)
  between operations  1.35 us (1%)
    ppermute x8, starting transfers between devices, passed_along(): return lax.ppermute(block, axis, route)  22.7 us
    all_to_all x2, waiting for transfers between devices, route(): lax.all_to_all(outbound, 'gz', split_axis=0, concat_axis=0, tiled=True)  13.9 us
    unnamed x122, local copies, waits for them, and re-layouts  12.3 us
    all_to_all x2, starting transfers between devices, route(): lax.all_to_all(outbound, 'gz', split_axis=0, concat_axis=0, tiled=True)  8.05 us
    ppermute x1, waiting for transfers between devices, from_behind(): return lax.ppermute(value, axis, pairs)  4.23 us
    slice x3, local copies, waits for them, and re-layouts, faces_of(): volume[:, :, extent - 1::extent].reshape(components, extent * extent)  2.23 us
    slice x3, local copies, waits for them, and re-layouts, faces_of(): low_z = volume[:, :, 0::extent].reshape(components, extent * extent)  2.16 us
  transfers between devices with their start and end apart: 11, of which 5 were waited for; matrix products, arithmetic and copies ran while one was open for 12% of the time, Pallas kernels for 0%

commit v1 on v0

v1 whole, which is shorter than its diff:
```python
import functools

import jax
import jax.numpy as jnp
from jax import lax
from jax.experimental import pallas as pl
from jax.experimental.pallas import tpu as pltpu
from jax.sharding import PartitionSpec as P

NPHASE = 4
STEPS = 2
LANES = 128
SEED_GAIN = 2.0
MESH = pl.DeviceIdType.MESH


def kernel(
    sizes,
    fields,
    seeds,
    coords,
    before,
    after,
    couple,
    latent,
    diffuse,
    gain,
    out,
    recv,
    seed_recv,
    vals,
    xsend,
    xghost,
    ysend,
    yghost,
    result,
    outbuf,
    in_send,
    in_recv,
    seed_send,
    seed_got,
    x_send,
    x_recv,
    y_send,
    y_recv,
    out_send,
    out_recv,
    local_sem,
):
    gx_n, gy_n, gz_n, nblk, cells, surface = sizes
    slots, nfield = outbuf.shape[1], outbuf.shape[2]
    rows = outbuf.shape[3]
    halves = surface // LANES
    per_column = vals.shape[1]
    x_parts = gz_n // halves
    gx, gy, gz = lax.axis_index("gx"), lax.axis_index("gy"), lax.axis_index("gz")
    odd_x, odd_y = gx % 2, gy % 2

    def part_of(g):
        a, b = g // halves, g % halves
        xh = a + odd_x * (x_parts - 1 - 2 * a)
        yh = b + odd_y * (halves - 1 - 2 * b)
        return xh, yh

    def window(ref, g):
        xh, yh = part_of(g)
        x0 = pl.multiple_of(xh * rows, rows)
        y0 = pl.multiple_of(yh * LANES, LANES)
        return ref.at[:, :, pl.ds(x0, rows), pl.ds(y0, LANES)]

    def seed_window(g):
        _, yh = part_of(g)
        return seeds.at[:, pl.ds(pl.multiple_of(yh * LANES, LANES), LANES)]

    xh, yh = part_of(gz)
    xpos = gx * x_parts + xh
    ypos = gy * halves + yh
    x_total, y_total = gx_n * x_parts, gy_n * halves
    dir_x = 1 - 2 * odd_x
    dir_y = 1 - 2 * odd_y
    xlo_in, xhi_in = xh > 0, xh < x_parts - 1
    ylo_in, yhi_in = yh > 0, yh < halves - 1
    sides = []
    for exists, inside, step_x, step_y, move in (
        (xpos > 0, xlo_in, -1, 0, -halves * dir_x),
        (xpos < x_total - 1, xhi_in, 1, 0, halves * dir_x),
        (ypos > 0, ylo_in, 0, -1, -dir_y),
        (ypos < y_total - 1, yhi_in, 0, 1, dir_y),
    ):
        ins = inside.astype(jnp.int32)
        device = (gx + step_x * (1 - ins), gy + step_y * (1 - ins), gz + move * ins)
        sides.append((exists, inside, device))

    barrier = pltpu.get_barrier_semaphore()
    for d in range(1, gz_n):
        pl.semaphore_signal(
            barrier, inc=1, device_id=(gx, gy, (gz + d) % gz_n), device_id_type=MESH
        )
    expected = gz_n - 1
    for exists, inside, device in sides:
        outside = jnp.logical_and(exists, jnp.logical_not(inside))

        @pl.when(outside)
        def _(device=device):
            pl.semaphore_signal(barrier, inc=1, device_id=device, device_id_type=MESH)

        expected = expected + outside.astype(jnp.int32)
    pl.semaphore_wait(barrier, expected)

    moves = []
    for d in range(gz_n - 1, 0, -1):
        to = (gz + d) % gz_n
        for src, dst, s_sem, r_sem in (
            (window(fields, to), recv.at[pl.ds(slots * gz, slots)], in_send, in_recv),
            (seed_window(to), seed_recv.at[gz], seed_send, seed_got),
        ):
            copy = pltpu.make_async_remote_copy(
                src_ref=src,
                dst_ref=dst,
                send_sem=s_sem.at[d - 1],
                recv_sem=r_sem.at[d - 1],
                device_id=(gx, gy, to),
                device_id_type=MESH,
            )
            copy.start()
            moves.append(copy)
    own = pltpu.make_async_copy(
        window(fields, gz), recv.at[pl.ds(slots * gz, slots)], local_sem.at[0]
    )
    own.start()
    own_seed = pltpu.make_async_copy(seed_window(gz), seed_recv.at[gz], local_sem.at[1])
    own_seed.start()

    base = (gx * gy_n + gy) * (gz_n * slots)
    places = gz_n * slots

    def lookup(b, carry):
        source, depth = carry
        here = jnp.logical_and(coords[0, b] == gx, coords[1, b] == gy)
        z = jnp.where(here, coords[2, b], -1)
        was = before[b] - base
        now = jnp.where(here, after[b] - base, -1)
        source = tuple(jnp.where(z == k, was, source[k]) for k in range(per_column))
        depth = tuple(jnp.where(now == q, z, depth[q]) for q in range(places))
        return source, depth

    source, depth = lax.fori_loop(
        0,
        nblk,
        lookup,
        ((jnp.int32(0),) * per_column, (jnp.int32(-1),) * places),
    )

    own.wait()
    own_seed.wait()
    for copy in moves:
        copy.wait()

    marks = []
    for k in range(per_column):
        p = source[k]
        vals[:, k] = recv[p]
        pair = seed_recv[p // slots]
        row = pair[0:1]
        for s in range(1, slots):
            row = jnp.where(p % slots == s, pair[s : s + 1], row)
        marks.append(row[None])
    marks = jnp.concatenate(marks, 0)

    shape = (per_column, rows, LANES)
    lane = lax.broadcasted_iota(jnp.int32, shape, 2)
    row_id = lax.broadcasted_iota(jnp.int32, shape, 1)
    z_cell = lane % cells
    group = lane // cells
    xglob = (row_id + (gx * cells + xh * rows)).astype(jnp.float32)

    def rolled(v, shift):
        shift = shift % LANES
        return v if shift == 0 else pltpu.roll(v, shift, 2)

    def exchange(step, old):
        low_y = jnp.zeros(shape, jnp.float32)
        high_y = low_y
        for f in range(nfield):
            v = old[f]
            xsend[step, 0, :, f : f + 1, :] = v[:, 0:1, :]
            xsend[step, 1, :, f : f + 1, :] = v[:, rows - 1 : rows, :]
            low_y = jnp.where(group == f, rolled(v, cells * f), low_y)
            high_y = jnp.where(group == f, rolled(v, cells * f + cells), high_y)
        ysend[step, 0] = low_y
        ysend[step, 1] = high_y
        for phase in ("start", "wait"):
            for side, (exists, _, device) in enumerate(sides):
                send, ghost, s_sem, r_sem = (
                    (xsend, xghost, x_send, x_recv)
                    if side < 2
                    else (ysend, yghost, y_send, y_recv)
                )
                e = side % 2

                @pl.when(exists)
                def _(send=send, ghost=ghost, s_sem=s_sem, r_sem=r_sem, e=e, device=device):
                    if phase == "start":
                        pltpu.make_async_remote_copy(
                            src_ref=send.at[step, e],
                            dst_ref=ghost.at[step, 1 - e],
                            send_sem=s_sem.at[step, e],
                            recv_sem=r_sem.at[step, 1 - e],
                            device_id=device,
                            device_id_type=MESH,
                        ).start()
                    else:
                        pltpu.make_async_remote_copy(
                            src_ref=send.at[step, e],
                            dst_ref=ghost.at[step, e],
                            send_sem=s_sem.at[step, e],
                            recv_sem=r_sem.at[step, e],
                            device_id=device,
                            device_id_type=MESH,
                        ).wait()

                if phase == "start":

                    @pl.when(jnp.logical_not(exists))
                    def _(send=send, ghost=ghost, e=e):
                        ghost[step, e] = send[step, e]

    def laplace(step, f, v):
        below_x = jnp.concatenate([xghost[step, 0, :, f : f + 1, :], v[:, :-1, :]], 1)
        above_x = jnp.concatenate([v[:, 1:, :], xghost[step, 1, :, f : f + 1, :]], 1)
        below_y = jnp.where(
            group == 0, rolled(yghost[step, 0], -cells * f), rolled(v, cells)
        )
        above_y = jnp.where(
            group == LANES // cells - 1,
            rolled(yghost[step, 1], -cells * f - cells),
            rolled(v, -cells),
        )
        before_k = jnp.concatenate([v[-1:], v[:-1]], 0)
        after_k = jnp.concatenate([v[1:], v[:1]], 0)
        below_z = jnp.where(z_cell == 0, rolled(before_k, 1 - cells), rolled(v, 1))
        above_z = jnp.where(z_cell == cells - 1, rolled(after_k, cells - 1), rolled(v, -1))
        return below_x + above_x + below_y + above_y + below_z + above_z - 6.0 * v

    for step in range(STEPS):
        src = vals if step == 0 else result.at[step - 1]
        exchange(step, [src[f] for f in range(nfield)])
        thermal = xglob / (2.0 * cells) - 1.0 - 0.25 * step
        change = []
        for k in range(NPHASE):
            phi = src[k]
            drive = gain[k] * thermal
            for j in range(nfield - NPHASE):
                drive = drive + couple[k, j] * src[NPHASE + j]
            if step == 0:
                drive = drive + SEED_GAIN * (marks == k).astype(jnp.float32)
            delta = 0.12 * laplace(step, k, phi) + phi * (1.0 - phi) * (phi - 0.5 + drive)
            new = phi + delta
            result[step, k] = new
            change.append(new - phi)
        for j in range(nfield - NPHASE):
            mu = src[NPHASE + j]
            new = mu + (0.1 * diffuse[j]) * laplace(step, NPHASE + j, mu)
            for k in range(NPHASE):
                new = new - latent[j, k] * change[k]
            result[step, NPHASE + j] = new

    for q in range(places):
        k = depth[q]
        tile = result[STEPS - 1, :, jnp.maximum(k, 0)]
        outbuf[q // slots, q % slots] = jnp.where(k >= 0, tile, 0.0)
    moves = []
    for d in range(gz_n - 1, 0, -1):
        to = (gz + d) % gz_n
        copy = pltpu.make_async_remote_copy(
            src_ref=outbuf.at[to],
            dst_ref=window(out, gz),
            send_sem=out_send.at[d - 1],
            recv_sem=out_recv.at[d - 1],
            device_id=(gx, gy, to),
            device_id_type=MESH,
        )
        copy.start()
        moves.append(copy)
    own = pltpu.make_async_copy(outbuf.at[gz], window(out, gz), local_sem.at[2])
    own.start()
    own.wait()
    for copy in moves:
        copy.wait()


def solution(mesh):
    gx_n, gy_n, gz_n = mesh.shape["gx"], mesh.shape["gy"], mesh.shape["gz"]

    def per_device(fields, seeds, coords, neighbours, before, after, couple, latent, diffuse, gain):
        slots, nfield, cells, surface = fields.shape
        nblk = coords.shape[0]
        per_column = nblk // (gx_n * gy_n)
        halves = surface // LANES
        rows = cells * halves // gz_n
        f32, i32 = jnp.float32, jnp.int32
        dma = pltpu.SemaphoreType.DMA
        smem = pl.BlockSpec(memory_space=pltpu.SMEM)
        anyspace = pl.BlockSpec(memory_space=pl.ANY)
        faces_x = (STEPS, 2, per_column, nfield, LANES)
        faces_y = (STEPS, 2, per_column, rows, LANES)
        return pl.pallas_call(
            functools.partial(kernel, (gx_n, gy_n, gz_n, nblk, cells, surface)),
            out_shape=jax.ShapeDtypeStruct(fields.shape, f32),
            in_specs=[anyspace, anyspace] + [smem] * 7,
            out_specs=anyspace,
            scratch_shapes=[
                pltpu.VMEM((gz_n * slots, nfield, rows, LANES), f32),
                pltpu.VMEM((gz_n, slots, LANES), i32),
                pltpu.VMEM((nfield, per_column, rows, LANES), f32),
                pltpu.VMEM(faces_x, f32),
                pltpu.VMEM(faces_x, f32),
                pltpu.VMEM(faces_y, f32),
                pltpu.VMEM(faces_y, f32),
                pltpu.VMEM((STEPS, nfield, per_column, rows, LANES), f32),
                pltpu.VMEM((gz_n, slots, nfield, rows, LANES), f32),
                dma((gz_n,)),
                dma((gz_n,)),
                dma((gz_n,)),
                dma((gz_n,)),
                dma((STEPS, 2)),
                dma((STEPS, 2)),
                dma((STEPS, 2)),
                dma((STEPS, 2)),
                dma((gz_n,)),
                dma((gz_n,)),
                dma((3,)),
            ],
            compiler_params=pltpu.CompilerParams(collective_id=0, has_side_effects=True),
        )(fields, seeds, coords.T, before, after, couple, latent, diffuse, gain)

    placed = (
        P(("gx", "gy", "gz"), None, None, None),
        P(("gx", "gy", "gz"), None),
    ) + (P(),) * 8
    return jax.shard_map(
        per_device,
        mesh=mesh,
        in_specs=placed,
        out_specs=P(("gx", "gy", "gz"), None, None, None),
        check_vma=False,
    )
```

time: 103 us -> 29.2 us (0.28)
  the two profiles are of different devices: /device:TPU:5 before, /device:TPU:0 now
where the time goes in v1:
time: 29.2 us; the launch traced here: 28.9 us
  Pallas kernels  27.3 us (93%)
  local copies, waits for them, and re-layouts  1.67 us (6%)
    pallas_call x1, Pallas kernels, per_device(): pl.pallas_call(functools.partial(kernel, (gx_n, gy_n, gz_n, nblk, cells,...  27.3 us
    unnamed x1, local copies, waits for them, and re-layouts  1.67 us

profile of v1, /device:TPU:0, one launch (start us, length us, event | category | flops | bytes accessed | tf_op | source)
XLA Modules:
  0.0 28.9 jit_solution(4720446486380928615)
XLA Ops:
  0.0 27.3 %shard_map.91 = f32[2,8,16,256]{3,2,1,0:T(8,128)} custom-call(f32[2,8,16,256]{3,2,1,0:T(8,128)} %fields.1, s32[2,256]{1,0:T(2,128)} %seeds.1, s32[3,48]{1,0:T(4,128)} %bitcast.1, s32[48]{0:T(128)} %before.1, s32[48]{0:T(128)} %after.1, f32[4,4]{1,0:T(4,128)} %couple.1, f32[4,4]{1,0:T(4,128)} %latent.1, f32[4]{0:T(128)} %diffuse.1, f32[4]{0:T(128)} %gain.1), custom_call_target="tpu_custom_call" | custom-call | tf_op jit(solution)/shard_map/pallas_call | solution.py:307
  27.3 1.7 %copy.11 = f32[2,8,16,256]{3,2,1,0:T(8,128)} copy(f32[2,8,16,256]{3,2,1,0:T(8,128)} %shard_map.91) | data formatting | bytes 524288
